TPU v7x, 32 devices: a whole 2x2x4 slice. The times are simulated.
32 devices in a mesh: head: 8 (over y, x, core), key: 4 (over z).
Axes of the slice: x: 2, y: 2, z: 4, core: 2. Of those that a mesh axis runs over, the one named last changes fastest.
Arguments:
- queries: bfloat16 [128, 128, 192], P(None, 'head'), may hold values from -16 to 16
- w_uk: bfloat16 [128, 128, 512], P('head'), may hold values from -0.5 to 0.5
- w_uv: bfloat16 [128, 512, 128], P('head'), may hold values from -0.25 to 0.25
- latent: bfloat16 [8192, 576], P('key'), may hold values from -5 to 5
- out_grad: bfloat16 [128, 128, 128], P(None, 'head'), may hold values from -6 to 6
- offsets: int32 [128], replicated, may hold values from 2048 to 8191, as said below
Outputs:
- d_queries: bfloat16 [128, 128, 192], P('key', 'head')
- d_latent: bfloat16 [8192, 576], P('key')
Inputs may be any that keep to these rules, and one draw needn't show every extreme that they name: Row r sees keys 0 to offsets[r].
All inputs are finite; a program needn't handle non-finite values.
Results may differ from a plain program's by a relative error of at most 0.0079.
Values may be sent and summed in bfloat16 or wider, within the bound.
A program may use at most 128 MiB of HBM per device.

v0:
```python
import math
import jax
import jax.numpy as jnp
from jax import lax
from jax.sharding import PartitionSpec as P

floor_score = -1e30


def joined(part, axis, combine):
    gathered = jax.tree.map(lambda a: lax.all_gather(a, axis), part)

    def take(source):
        return jax.tree.map(lambda a: lax.dynamic_index_in_dim(a, source, 0, False), gathered)

    return lax.fori_loop(
        1, lax.axis_size(axis), lambda source, state: combine(state, take(source)), take(0)
    )


def combine_norms(earlier, later):
    top = jnp.maximum(earlier[0], later[0])
    total = earlier[1] * jnp.exp(earlier[0] - top) + later[1] * jnp.exp(later[0] - top)
    return (top, total)


def shards(queries, w_uk, w_uv, latent, out_grad, offsets):
    rows, heads, width = queries.shape
    keys = latent.shape[0]
    nope_width = w_uk.shape[1]
    lat_width = w_uk.shape[2]
    scale = 1.0 / math.sqrt(width)
    q_lat = jnp.einsum(
        "rhd,hdc->rhc", queries[:, :, :nope_width], w_uk, preferred_element_type=jnp.float32
    ).astype(jnp.bfloat16)
    q_cat = jnp.concatenate([q_lat, queries[:, :, nope_width:]], axis=2)
    d_lat = jnp.einsum("rhe,hce->rhc", out_grad, w_uv, preferred_element_type=jnp.float32).astype(
        jnp.bfloat16
    )
    scores = jnp.einsum("rhc,kc->hrk", q_cat, latent, preferred_element_type=jnp.float32) * scale
    position = lax.axis_index("key") * keys + jnp.arange(keys, dtype=jnp.int32)
    visible = (position[None, :] <= offsets[:, None])[None]
    masked = jnp.where(visible, scores, floor_score)
    local_top = jnp.max(masked, axis=2)
    local_total = jnp.sum(jnp.where(visible, jnp.exp(masked - local_top[..., None]), 0.0), axis=2)
    top, total = joined((local_top, local_total), "key", combine_norms)
    log_norm = top + jnp.log(total)
    probs = jnp.where(visible, jnp.exp(masked - log_norm[..., None]), 0.0)
    d_probs = jnp.einsum(
        "rhc,kc->hrk", d_lat, latent[:, :lat_width], preferred_element_type=jnp.float32
    )
    delta = lax.psum(jnp.sum(probs * d_probs, axis=2), "key")
    d_scores = (probs * (d_probs - delta[..., None])).astype(jnp.bfloat16)
    probs_b = probs.astype(jnp.bfloat16)
    up_key = w_uk.astype(jnp.float32)
    part_sum = (
        jnp.einsum("hrk,kc->rhc", d_scores, latent, preferred_element_type=jnp.float32) * scale
    )
    nope = jnp.einsum(
        "rhc,hdc->rhd", part_sum[..., :lat_width], up_key, precision=lax.Precision.HIGHEST
    )
    dq_sum = lax.psum_scatter(
        jnp.concatenate([nope, part_sum[..., lat_width:]], axis=2),
        "key",
        scatter_dimension=0,
        tiled=True,
    )
    d_queries = dq_sum.astype(jnp.bfloat16)
    from_scores = (
        jnp.einsum("hrk,rhc->kc", d_scores, q_cat, preferred_element_type=jnp.float32) * scale
    )
    from_values = jnp.einsum("hrk,rhc->kc", probs_b, d_lat, preferred_element_type=jnp.float32)
    d_latent = lax.psum(
        jnp.concatenate(
            [from_scores[:, :lat_width] + from_values, from_scores[:, lat_width:]], axis=1
        ),
        "head",
    ).astype(jnp.bfloat16)
    return (d_queries, d_latent)


def solution(mesh):
    return jax.shard_map(
        shards,
        mesh=mesh,
        in_specs=(
            P(None, "head", None),
            P("head", None, None),
            P("head", None, None),
            P("key", None),
            P(None, "head", None),
            P(),
        ),
        out_specs=(P("key", "head", None), P("key", None)),
        check_vma=False,
    )
```

profile of v0, /device:TPU:0, one launch (start us, length us, event | category | flops | bytes accessed | tf_op | source)
XLA Modules:
  0.0 233.1 jit_solution(15037375372007042544)
XLA Ops:
  7.2 0.0 reduce-scatter.2.cloned.1.call-start
  7.3 1.1 slice.24
  8.4 0.4 copy-done
  8.8 1.8 convert_bitcast_fusion
  10.7 0.2 broadcast_compare_fusion
  10.9 8.4 %bitcast_reduce_fusion = (f32[16,128]{1,0:T(8,128)S(1)}, f32[128,16,2048]{2,0,1:T(8,128)S(1)}) fusion(pred[128,2048]{1,0:T(8,128)(4,1)S(1)} %broadcast_compare_fusion, bf16[2048,576]{0,1:T(8,128)(2,1)S(1)} %copy-done.9, bf16[128,16,64]{0,2,1:T(8,128)(2,1)S(1)} %slice.24, bf16[128,16,512]{0,2,1:T(8,128)(2,1)S(1)} %convert_bitcast_fusion), kind=kOutput, calls=%fused_computation.12 | convolution fusion | flops 4849137664 | bytes 21766144 | tf_op jit(solution)/shard_map/rhc,kc->hrk/dot_general | solution.py:40
  19.3 14.8 %all-gather = f32[64,128]{1,0:T(8,128)S(1)} all-gather(f32[16,128]{1,0:T(8,128)S(1)} %get-tuple-element.151), channel_id=2, replica_groups=mesh['head'=8,'key'=4] {'key'}, dimensions={0}, use_global_device_ids=true | all-gather | bytes 40960 | tf_op jit(solution)/shard_map/all_gather | solution.py:11
  34.1 5.0 %fusion.7 = f32[16,128]{1,0:T(8,128)S(1)} fusion(f32[128,16,2048]{2,0,1:T(8,128)S(1)} %get-tuple-element.152, f32[16,128]{1,0:T(8,128)S(1)} %get-tuple-element.151, pred[128,2048]{1,0:T(8,128)(4,1)S(1)} %broadcast_compare_fusion), kind=kLoop, calls=%fused_computation.15 | loop fusion | flops 20969472 | bytes 17055744 | tf_op jit(solution)/shard_map/reduce_sum | solution.py:45
  39.2 13.3 %all-gather.1 = f32[64,128]{1,0:T(8,128)S(1)} all-gather(f32[16,128]{1,0:T(8,128)S(1)} %fusion.7), channel_id=3, replica_groups=mesh['head'=8,'key'=4] {'key'}, dimensions={0}, use_global_device_ids=true | all-gather | bytes 40960 | tf_op jit(solution)/shard_map/all_gather | solution.py:11
  52.6 0.1 while.17
  52.7 2.5 %convolution_convert_fusion = bf16[16,512,128]{2,1,0:T(8,128)(2,1)S(1)} fusion(bf16[16,512,128]{2,1,0:T(8,128)(2,1)} %param.10, bf16[128,16,128]{2,1,0:T(8,128)(2,1)S(1)} %copy-done.7), kind=kOutput, calls=%fused_computation.38 | convolution fusion | flops 269484032 | bytes 4718592 | tf_op jit(solution)/shard_map/rhe,hce->rhc/dot_general | solution.py:37
  55.2 16.4 %fusion.2 = (f32[16,128]{1,0:T(8,128)S(1)}, f32[128,16,2048]{2,0,1:T(8,128)}) fusion(f32[16,128]{1,0:T(8,128)S(1)} %log_add_fusion, f32[128,16,2048]{2,0,1:T(8,128)} %copy-done.2, pred[128,2048]{1,0:T(8,128)(4,1)S(1)} %broadcast_compare_fusion, bf16[2048,576]{0,1:T(8,128)(2,1)S(1)} %copy-done.10, bf16[16,512,128]{2,1,0:T(8,128)(2,1)S(1)} %convolution_convert_fusion), kind=kOutput, calls=%fused_computation.7 | convolution fusion | flops 4320131072 | bytes 38289408 | tf_op jit(solution)/shard_map/rhc,kc->hrk/dot_general | solution.py:49
  71.6 11.8 %psum.14 = f32[16,128]{1,0:T(8,128)S(1)} all-reduce(f32[16,128]{1,0:T(8,128)S(1)} %get-tuple-element.153), channel_id=1, replica_groups=mesh['head'=8,'key'=4] {'key'}, use_global_device_ids=true, to_apply=%region_5.6 | all-reduce | flops 2048 | bytes 16384 | tf_op jit(solution)/shard_map/psum | solution.py:52
  83.5 13.1 %fusion.4 = bf16[16,128,2048]{2,1,0:T(8,128)(2,1)S(1)} fusion(f32[128,16,2048]{2,0,1:T(8,128)} %get-tuple-element.154, f32[16,128]{1,0:T(8,128)S(1)} %psum.14, f32[16,128]{1,0:T(8,128)S(1)} %log_add_fusion, f32[128,16,2048]{2,0,1:T(8,128)} %copy-done.2, pred[128,2048]{1,0:T(8,128)(4,1)S(1)} %broadcast_compare_fusion), kind=kLoop, calls=%fused_computation.9 | loop fusion | flops 29360128 | bytes 42221568 | tf_op jit(solution)/shard_map/convert_element_type | solution.py:53
  96.6 5.1 %multiply_bitcast_fusion = f32[128,16,576]{0,2,1:T(8,128)S(1)} fusion(bf16[16,128,2048]{2,1,0:T(8,128)(2,1)S(1)} %fusion.4, bf16[2048,576]{0,1:T(8,128)(2,1)S(1)} %copy-done.11), kind=kOutput, calls=%fused_computation.23 | convolution fusion | flops 4833017856 | bytes 15466496 | tf_op jit(solution)/shard_map/hrk,kc->rhc/dot_general | solution.py:57
  101.8 2.5 %fusion.28 = f32[128,16,128]{0,2,1:T(8,128)S(1)} fusion(bf16[16,128,512]{2,1,0:T(8,128)(2,1)S(1)} %copy-done, f32[128,16,576]{0,2,1:T(8,128)S(1)} %multiply_bitcast_fusion), kind=kOutput, calls=%fused_computation.40 | convolution fusion | flops 1610612736 | bytes 7340032 | tf_op jit(solution)/shard_map/rhc,hdc->rhd/dot_general | solution.py:59
  104.3 0.1 pad_maximum_fusion.2
  104.4 2.0 copy.21
  106.4 0.0 reduce-scatter.2.cloned.1.call-update
  106.5 8.3 %bitcast_multiply_fusion.2 = f32[2048,576]{0,1:T(8,128)S(1)} fusion(bf16[16,128,2048]{2,1,0:T(8,128)(2,1)} %copy-done.3, bf16[128,16,64]{0,2,1:T(8,128)(2,1)S(1)} %slice.24, bf16[128,16,512]{0,2,1:T(8,128)(2,1)} %copy-done.4), kind=kOutput, calls=%fused_computation.22 | convolution fusion | flops 4837736448 | bytes 15466496 | tf_op jit(solution)/shard_map/hrk,rhc->kc/dot_general | solution.py:70
  114.7 9.0 %slice_add_fusion = f32[2048,512]{0,1:T(8,128)S(1)} fusion(f32[2048,576]{0,1:T(8,128)S(1)} %bitcast_multiply_fusion.2, f32[16,128]{1,0:T(8,128)S(1)} %log_add_fusion, f32[128,16,2048]{2,0,1:T(8,128)} %copy-done.2, pred[128,2048]{1,0:T(8,128)(4,1)S(1)} %broadcast_compare_fusion, bf16[16,512,128]{2,1,0:T(8,128)(2,1)S(1)} %copy-done.6), kind=kOutput, calls=%fused_computation.24 | convolution fusion | flops 4316987392 | bytes 27795456 | tf_op jit(solution)/shard_map/hrk,rhc->kc/dot_general | solution.py:72
  123.8 2.4 %pad_maximum_fusion = f32[2048,576]{0,1:T(8,128)} fusion(f32[2048,64]{0,1:T(8,128)S(1)} %slice.37, f32[2048,512]{0,1:T(8,128)S(1)} %slice_add_fusion), kind=kLoop, calls=%fused_computation.21 | loop fusion | flops 1179648 | bytes 9437184 | tf_op jit(solution)/shard_map/concatenate | solution.py:74
  126.2 98.2 %all-reduce.1 = bf16[2048,576]{0,1:T(8,128)(2,1)} all-reduce(f32[2048,576]{0,1:T(8,128)} %pad_maximum_fusion), channel_id=1, replica_groups=mesh['head'=8,'key'=4] {'head'}, use_global_device_ids=true, to_apply=%region_7.8 | all-reduce | flops 1179648 | bytes 7077888 | tf_op jit(solution)/shard_map/psum | solution.py:73
  224.5 1.8 convert_element_type.30
  (33 shorter events, 0.2 us)
Async XLA Ops:
  7.2 1.7 copy-start
  7.2 3.5 %copy-start.8 = (s32[128]{0:T(128)S(1)}, s32[128]{0:T(128)}, u32[]{:S(2)}) copy-start(s32[128]{0:T(128)} %param.13) | copy-start | bytes 1540
  7.2 217.3 %reduce-scatter.2.cloned.1.call-start = ((), (), s32[]{:S(2)}) async-start(), calls=%async_computation.1 | async-start | bytes 2621440 | tf_op jit(solution)/shard_map/reduce_scatter | solution.py:62
  7.2 3.7 %copy-start.9 = (bf16[2048,576]{0,1:T(8,128)(2,1)S(1)}, bf16[2048,576]{0,1:T(8,128)(2,1)}, u32[]{:S(2)}) copy-start(bf16[2048,576]{0,1:T(8,128)(2,1)} %param.11) | copy-start | bytes 7077892
  10.7 8.6 %copy-start.4 = (bf16[128,16,512]{0,2,1:T(8,128)(2,1)}, bf16[128,16,512]{0,2,1:T(8,128)(2,1)S(1)}, u32[]{:S(2)}) copy-start(bf16[128,16,512]{0,2,1:T(8,128)(2,1)S(1)} %convert_bitcast_fusion) | copy-start | bytes 6291460
  19.3 19.9 %copy-start.2 = (f32[128,16,2048]{2,0,1:T(8,128)}, f32[128,16,2048]{2,0,1:T(8,128)S(1)}, u32[]{:S(2)}) copy-start(f32[128,16,2048]{2,0,1:T(8,128)S(1)} %get-tuple-element.152) | copy-start | bytes 50331652
  34.1 18.5 %copy-start.7 = (bf16[128,16,128]{2,1,0:T(8,128)(2,1)S(1)}, bf16[128,16,128]{2,1,0:T(8,128)(2,1)}, u32[]{:S(2)}) copy-start(bf16[128,16,128]{2,1,0:T(8,128)(2,1)} %param.12) | copy-start | bytes 1572868
  52.7 2.5 %copy-start.10 = (bf16[2048,576]{0,1:T(8,128)(2,1)S(1)}, bf16[2048,576]{0,1:T(8,128)(2,1)}, u32[]{:S(2)}) copy-start(bf16[2048,576]{0,1:T(8,128)(2,1)} %param.11) | copy-start | bytes 7077892
  55.2 16.5 %copy-start.5 = (bf16[16,512,128]{2,1,0:T(8,128)(2,1)}, bf16[16,512,128]{2,1,0:T(8,128)(2,1)S(1)}, u32[]{:S(2)}) copy-start(bf16[16,512,128]{2,1,0:T(8,128)(2,1)S(1)} %convolution_convert_fusion) | copy-start | bytes 6291460
  83.5 13.2 %copy-start.11 = (bf16[2048,576]{0,1:T(8,128)(2,1)S(1)}, bf16[2048,576]{0,1:T(8,128)(2,1)}, u32[]{:S(2)}) copy-start(bf16[2048,576]{0,1:T(8,128)(2,1)} %param.11) | copy-start | bytes 7077892
  96.6 5.1 %copy-start.3 = (bf16[16,128,2048]{2,1,0:T(8,128)(2,1)}, bf16[16,128,2048]{2,1,0:T(8,128)(2,1)S(1)}, u32[]{:S(2)}) copy-start(bf16[16,128,2048]{2,1,0:T(8,128)(2,1)S(1)} %fusion.4) | copy-start | bytes 25165828
  106.5 8.3 %copy-start.6 = (bf16[16,512,128]{2,1,0:T(8,128)(2,1)S(1)}, bf16[16,512,128]{2,1,0:T(8,128)(2,1)}, u32[]{:S(2)}) copy-start(bf16[16,512,128]{2,1,0:T(8,128)(2,1)} %copy-done.5) | copy-start | bytes 6291460
  123.8 102.5 %copy-start.1 = (bf16[16,128,512]{2,1,0:T(8,128)(2,1)S(1)}, bf16[16,128,512]{2,1,0:T(8,128)(2,1)}, u32[]{:S(2)}) copy-start(bf16[16,128,512]{2,1,0:T(8,128)(2,1)} %param.9) | copy-start | bytes 6291460
Sparse Core Ops, SparseCore 0:
  106.6 41.8 reduce-scatter.1
where the time goes:
time: 233 us
  blocking collectives  138 us (59%)
  matrix products  53.9 us (23%)
  other arithmetic  22.8 us (10%)
  between operations  14.3 us (6%)
  local copies, waits for them, and re-layouts  3.72 us (2%)
    psum x1, blocking collectives, shards(): lax.psum(jnp.concatenate([from_scores[:, :lat_width] + from_values, from_...  98.2 us
    all_gather x2, blocking collectives, joined(): gathered = jax.tree.map(lambda a: lax.all_gather(a, axis), part)  28.2 us
    dot_general x1, matrix products, shards(): jnp.einsum('rhc,kc->hrk', d_lat, latent[:, :lat_width], preferred_element...  16.4 us
    convert_element_type x1, other arithmetic, shards(): d_scores = (probs * (d_probs - delta[..., None])).astype(jnp.bfloat16)  13.1 us
    psum x1, blocking collectives, shards(): delta = lax.psum(jnp.sum(probs * d_probs, axis=2), 'key')  11.8 us
    dot_general x1, matrix products, shards(): jnp.einsum('hrk,rhc->kc', probs_b, d_lat, preferred_element_type=jnp.floa...  9.01 us
    dot_general x1, matrix products, shards(): jnp.einsum('rhc,kc->hrk', q_cat, latent, preferred_element_type=jnp.float32)  8.36 us
    dot_general x1, matrix products, shards(): jnp.einsum('hrk,rhc->kc', d_scores, q_cat, preferred_element_type=jnp.flo...  8.25 us
  transfers between devices with their start and end apart: 1, of which 0 were waited for; matrix products, arithmetic and copies ran while one was open for 8% of the time, Pallas kernels for 0%

commit v1 on v0

--- a/solution.py
+++ b/solution.py
@@ -70,11 +70,14 @@
         jnp.einsum("hrk,rhc->kc", d_scores, q_cat, preferred_element_type=jnp.float32) * scale
     )
     from_values = jnp.einsum("hrk,rhc->kc", probs_b, d_lat, preferred_element_type=jnp.float32)
-    d_latent = lax.psum(
-        jnp.concatenate(
-            [from_scores[:, :lat_width] + from_values, from_scores[:, lat_width:]], axis=1
+    d_latent = jnp.sum(
+        lax.all_gather(
+            jnp.concatenate(
+                [from_scores[:, :lat_width] + from_values, from_scores[:, lat_width:]], axis=1
+            ),
+            "head",
         ),
-        "head",
+        axis=0,
     ).astype(jnp.bfloat16)
     return (d_queries, d_latent)
 

time: 233 us -> 365 us (1.57)
  waiting for transfers between devices: 0.02 us -> 176 us
  blocking collectives: 138 us -> 40 us
  local copies, waits for them, and re-layouts: 3.72 us -> 40.5 us
  other arithmetic: 22.8 us -> 38 us
    all_gather x0 -> x1, waiting for transfers between devices: none -> 154 us  [shards(): lax.all_gather(jnp.concatenate([from_scores[:, :lat_width] + from_values,...]
    psum x1 -> x0, blocking collectives: 98.2 us -> none  [shards(): lax.psum(jnp.concatenate([from_scores[:, :lat_width] + from_values, from_...]
    unnamed x24 -> x25, local copies, waits for them, and re-layouts: 0.51 us -> 37.4 us
    reduce_scatter x1, waiting for transfers between devices: 0.01 us -> 21.7 us  [shards(): lax.psum_scatter(jnp.concatenate([nope, part_sum[..., lat_width:]], axis=...]
    reduce_sum x0 -> x1, other arithmetic: none -> 15.2 us  [shards(): jnp.sum(lax.all_gather(jnp.concatenate([from_scores[:, :lat_width] + from...]
  transfers between devices with their start and end apart: 1 -> 2, of which waited for: 0 -> 2; matrix products, arithmetic and copies ran while one was open for 8% -> 6% of each run, Pallas kernels for 0% -> 0%
where the time goes in v1:
time: 365 us
  waiting for transfers between devices  176 us (48%)
  matrix products  54.1 us (15%)
  local copies, waits for them, and re-layouts  40.5 us (11%)
  blocking collectives  40 us (11%)
  other arithmetic  38 us (10%)
  between operations  15.8 us (4%)
    all_gather x1, waiting for transfers between devices, shards(): lax.all_gather(jnp.concatenate([from_scores[:, :lat_width] + from_values,...  154 us
    unnamed x25, local copies, waits for them, and re-layouts  37.4 us
    all_gather x2, blocking collectives, joined(): gathered = jax.tree.map(lambda a: lax.all_gather(a, axis), part)  28.2 us
    reduce_scatter x1, waiting for transfers between devices, shards(): lax.psum_scatter(jnp.concatenate([nope, part_sum[..., lat_width:]], axis=...  21.7 us
    dot_general x1, matrix products, shards(): jnp.einsum('rhc,kc->hrk', d_lat, latent[:, :lat_width], preferred_element...  16.5 us
    reduce_sum x1, other arithmetic, shards(): jnp.sum(lax.all_gather(jnp.concatenate([from_scores[:, :lat_width] + from...  15.2 us
    convert_element_type x1, other arithmetic, shards(): d_scores = (probs * (d_probs - delta[..., None])).astype(jnp.bfloat16)  13.1 us
    psum x1, blocking collectives, shards(): delta = lax.psum(jnp.sum(probs * d_probs, axis=2), 'key')  11.8 us
  transfers between devices with their start and end apart: 2, of which 2 were waited for; matrix products, arithmetic and copies ran while one was open for 6% of the time, Pallas kernels for 0%

profile of v1, /device:TPU:0, one launch (start us, length us, event | category | flops | bytes accessed | tf_op | source)
XLA Modules:
  0.0 364.7 jit_solution(11518773208361324322)
XLA Ops:
  8.1 1.1 slice.24
  9.2 0.4 copy-done
  9.7 1.8 convert_bitcast_fusion
  11.5 0.2 broadcast_compare_fusion
  11.7 8.4 %bitcast_reduce_fusion.1 = (f32[16,128]{1,0:T(8,128)S(1)}, f32[128,16,2048]{2,0,1:T(8,128)S(1)}) fusion(pred[128,2048]{1,0:T(8,128)(4,1)S(1)} %broadcast_compare_fusion, bf16[2048,576]{0,1:T(8,128)(2,1)S(1)} %copy-done.9, bf16[128,16,64]{0,2,1:T(8,128)(2,1)S(1)} %slice.24, bf16[128,16,512]{0,2,1:T(8,128)(2,1)S(1)} %convert_bitcast_fusion), kind=kOutput, calls=%fused_computation.13 | convolution fusion | flops 4849137664 | bytes 21766144 | tf_op jit(solution)/shard_map/rhc,kc->hrk/dot_general | solution.py:40
  20.1 14.8 %all-gather = f32[64,128]{1,0:T(8,128)S(1)} all-gather(f32[16,128]{1,0:T(8,128)S(1)} %get-tuple-element.151), channel_id=2, replica_groups=mesh['head'=8,'key'=4] {'key'}, dimensions={0}, use_global_device_ids=true | all-gather | bytes 40960 | tf_op jit(solution)/shard_map/all_gather | solution.py:11
  35.0 5.0 %fusion.7 = f32[16,128]{1,0:T(8,128)S(1)} fusion(f32[128,16,2048]{2,0,1:T(8,128)S(1)} %get-tuple-element.152, f32[16,128]{1,0:T(8,128)S(1)} %get-tuple-element.151, pred[128,2048]{1,0:T(8,128)(4,1)S(1)} %broadcast_compare_fusion), kind=kLoop, calls=%fused_computation.16 | loop fusion | flops 20969472 | bytes 17055744 | tf_op jit(solution)/shard_map/reduce_sum | solution.py:45
  40.0 13.3 %all-gather.1 = f32[64,128]{1,0:T(8,128)S(1)} all-gather(f32[16,128]{1,0:T(8,128)S(1)} %fusion.7), channel_id=3, replica_groups=mesh['head'=8,'key'=4] {'key'}, dimensions={0}, use_global_device_ids=true | all-gather | bytes 40960 | tf_op jit(solution)/shard_map/all_gather | solution.py:11
  53.5 2.5 convolution_convert_fusion
  56.0 16.5 %fusion.2 = (f32[16,128]{1,0:T(8,128)S(1)}, f32[128,16,2048]{2,0,1:T(8,128)}) fusion(f32[16,128]{1,0:T(8,128)S(1)} %log_add_fusion, f32[128,16,2048]{2,0,1:T(8,128)} %copy-done.2, pred[128,2048]{1,0:T(8,128)(4,1)S(1)} %broadcast_compare_fusion, bf16[2048,576]{0,1:T(8,128)(2,1)S(1)} %copy-done.10, bf16[16,512,128]{2,1,0:T(8,128)(2,1)S(1)} %convolution_convert_fusion), kind=kOutput, calls=%fused_computation.8 | convolution fusion | flops 4320131072 | bytes 38289408 | tf_op jit(solution)/shard_map/rhc,kc->hrk/dot_general | solution.py:49
  72.5 11.8 %psum.7 = f32[16,128]{1,0:T(8,128)S(1)} all-reduce(f32[16,128]{1,0:T(8,128)S(1)} %get-tuple-element.153), channel_id=1, replica_groups=mesh['head'=8,'key'=4] {'key'}, use_global_device_ids=true, to_apply=%region_5.6 | all-reduce | flops 2048 | bytes 16384 | tf_op jit(solution)/shard_map/psum | solution.py:52
  84.3 13.1 %fusion.4 = bf16[16,128,2048]{2,1,0:T(8,128)(2,1)S(1)} fusion(f32[128,16,2048]{2,0,1:T(8,128)} %get-tuple-element.154, f32[16,128]{1,0:T(8,128)S(1)} %psum.7, f32[16,128]{1,0:T(8,128)S(1)} %log_add_fusion, f32[128,16,2048]{2,0,1:T(8,128)} %copy-done.2, pred[128,2048]{1,0:T(8,128)(4,1)S(1)} %broadcast_compare_fusion), kind=kLoop, calls=%fused_computation.10 | loop fusion | flops 29360128 | bytes 42221568 | tf_op jit(solution)/shard_map/convert_element_type | solution.py:53
  97.5 5.1 %multiply_bitcast_fusion = f32[128,16,576]{0,2,1:T(8,128)S(1)} fusion(bf16[16,128,2048]{2,1,0:T(8,128)(2,1)S(1)} %fusion.4, bf16[2048,576]{0,1:T(8,128)(2,1)S(1)} %copy-done.11), kind=kOutput, calls=%fused_computation.24 | convolution fusion | flops 4833017856 | bytes 15466496 | tf_op jit(solution)/shard_map/hrk,kc->rhc/dot_general | solution.py:57
  102.6 2.5 fusion.28
  105.3 1.9 copy.21
  107.2 0.3 all-gather.5.cloned.1.call-start
  107.5 8.3 %bitcast_multiply_fusion.2 = f32[2048,576]{0,1:T(8,128)S(1)} fusion(bf16[16,128,2048]{2,1,0:T(8,128)(2,1)} %copy-done.3, bf16[128,16,64]{0,2,1:T(8,128)(2,1)S(1)} %slice.24, bf16[128,16,512]{0,2,1:T(8,128)(2,1)} %copy-done.4), kind=kOutput, calls=%fused_computation.23 | convolution fusion | flops 4837736448 | bytes 15466496 | tf_op jit(solution)/shard_map/hrk,rhc->kc/dot_general | solution.py:70
  115.8 9.2 %slice_add_fusion = f32[2048,512]{0,1:T(8,128)S(1)} fusion(f32[2048,576]{0,1:T(8,128)S(1)} %bitcast_multiply_fusion.2, f32[16,128]{1,0:T(8,128)S(1)} %log_add_fusion, f32[128,16,2048]{2,0,1:T(8,128)} %copy-done.2, pred[128,2048]{1,0:T(8,128)(4,1)S(1)} %broadcast_compare_fusion, bf16[16,512,128]{2,1,0:T(8,128)(2,1)S(1)} %copy-done.6), kind=kOutput, calls=%fused_computation.25 | convolution fusion | flops 4316987392 | bytes 27795456 | tf_op jit(solution)/shard_map/hrk,rhc->kc/dot_general | solution.py:72
  125.0 2.5 pad_maximum_fusion
  127.5 21.7 %reduce-scatter.2.cloned.1.call-done = f32[32,16,192]{2,1,0:T(8,128)} async-done(((f32[128,16,192]{2,1,0:T(8,128)}), f32[32,16,192]{2,1,0:T(8,128)}) %reduce-scatter.2.cloned.1.call-update) | async-done | bytes 393232 | tf_op jit(solution)/shard_map/reduce_scatter | solution.py:62
  149.2 1.8 convert_element_type.30
  151.0 154.2 %all-gather.5.cloned.1.call-done = f32[16384,576]{0,1:T(8,128)} async-done(((f32[2048,576]{0,1:T(8,128)}), f32[16384,576]{0,1:T(8,128)}) %all-gather.5.cloned.1.call-update) | async-done | bytes 37748752 | tf_op jit(solution)/shard_map/all_gather | solution.py:74
  305.2 36.9 %copy.27 = f32[72,8,8,2048]{3,2,1,0:T(8,128)} copy(f32[72,8,8,2048]{3,1,2,0:T(8,128)} %bitcast.90) | data formatting | bytes 75497472
  342.1 15.2 %bitcast_reduce_fusion = bf16[2048,576]{0,1:T(8,128)(2,1)} fusion(f32[72,8,8,2048]{3,2,1,0:T(8,128)} %copy.27), kind=kLoop, calls=%fused_computation.5 | loop fusion | flops 8257536 | bytes 40108032 | tf_op jit(solution)/shard_map/reduce_sum | solution.py:73
  (37 shorter events, 0.5 us)
Async XLA Ops:
  8.0 1.7 copy-start
  8.0 3.5 copy-start.8
  8.0 141.2 %reduce-scatter.2.cloned.1.call-start = ((), (), s32[]{:S(2)}) async-start(), calls=%async_computation.1 | async-start | bytes 2621440 | tf_op jit(solution)/shard_map/reduce_scatter | solution.py:62
  8.1 3.7 %copy-start.9 = (bf16[2048,576]{0,1:T(8,128)(2,1)S(1)}, bf16[2048,576]{0,1:T(8,128)(2,1)}, u32[]{:S(2)}) copy-start(bf16[2048,576]{0,1:T(8,128)(2,1)} %param.11) | copy-start | bytes 7077892
  11.5 8.6 %copy-start.4 = (bf16[128,16,512]{0,2,1:T(8,128)(2,1)}, bf16[128,16,512]{0,2,1:T(8,128)(2,1)S(1)}, u32[]{:S(2)}) copy-start(bf16[128,16,512]{0,2,1:T(8,128)(2,1)S(1)} %convert_bitcast_fusion) | copy-start | bytes 6291460
  20.1 19.9 %copy-start.2 = (f32[128,16,2048]{2,0,1:T(8,128)}, f32[128,16,2048]{2,0,1:T(8,128)S(1)}, u32[]{:S(2)}) copy-start(f32[128,16,2048]{2,0,1:T(8,128)S(1)} %get-tuple-element.152) | copy-start | bytes 50331652
  35.0 18.5 %copy-start.7 = (bf16[128,16,128]{2,1,0:T(8,128)(2,1)S(1)}, bf16[128,16,128]{2,1,0:T(8,128)(2,1)}, u32[]{:S(2)}) copy-start(bf16[128,16,128]{2,1,0:T(8,128)(2,1)} %param.12) | copy-start | bytes 1572868
  53.5 2.5 copy-start.10
  56.0 16.5 %copy-start.5 = (bf16[16,512,128]{2,1,0:T(8,128)(2,1)}, bf16[16,512,128]{2,1,0:T(8,128)(2,1)S(1)}, u32[]{:S(2)}) copy-start(bf16[16,512,128]{2,1,0:T(8,128)(2,1)S(1)} %convolution_convert_fusion) | copy-start | bytes 6291460
  84.3 13.1 %copy-start.11 = (bf16[2048,576]{0,1:T(8,128)(2,1)S(1)}, bf16[2048,576]{0,1:T(8,128)(2,1)}, u32[]{:S(2)}) copy-start(bf16[2048,576]{0,1:T(8,128)(2,1)} %param.11) | copy-start | bytes 7077892
  97.5 5.1 %copy-start.3 = (bf16[16,128,2048]{2,1,0:T(8,128)(2,1)}, bf16[16,128,2048]{2,1,0:T(8,128)(2,1)S(1)}, u32[]{:S(2)}) copy-start(bf16[16,128,2048]{2,1,0:T(8,128)(2,1)S(1)} %fusion.4) | copy-start | bytes 25165828
  107.2 198.0 %all-gather.5.cloned.1.call-start = ((), (), s32[]{:S(2)}) async-start(), calls=%async_computation.2 | async-start | bytes 42467328 | tf_op jit(solution)/shard_map/all_gather | solution.py:74
  107.5 8.3 %copy-start.6 = (bf16[16,512,128]{2,1,0:T(8,128)(2,1)S(1)}, bf16[16,512,128]{2,1,0:T(8,128)(2,1)}, u32[]{:S(2)}) copy-start(bf16[16,512,128]{2,1,0:T(8,128)(2,1)} %copy-done.5) | copy-start | bytes 6291460
  342.1 15.2 %copy-start.1 = (bf16[16,128,512]{2,1,0:T(8,128)(2,1)S(1)}, bf16[16,128,512]{2,1,0:T(8,128)(2,1)}, u32[]{:S(2)}) copy-start(bf16[16,128,512]{2,1,0:T(8,128)(2,1)} %param.9) | copy-start | bytes 6291460
Sparse Core Ops, SparseCore 0:
  107.3 41.8 reduce-scatter.1
Sparse Core Ops, SparseCore 1:
  127.6 177.5 all-gather.4
